TPU v7x, 32 devices: a whole 2x2x4 slice. The times are simulated.
32 devices in a mesh: img: 8 (over y, x, core), seq: 4 (over z).
Axes of the slice: x: 2, y: 2, z: 4, core: 2. Of those that a mesh axis runs over, the one named last changes fastest.
Arguments:
- x_big: bfloat16 [128, 200, 768], P(('img', 'seq')), may hold values from -6 to 6
- x_small: bfloat16 [512, 40, 768], P(('img', 'seq')), may hold values from -6 to 6
- mask_big: int32 [128, 200], P('img'), may hold values from 0 to 1, as said below
- mask_small: int32 [512, 40], P('img'), may hold values from 0 to 1, as said below
- ln1_gain: float32 [768], P('seq'), may hold values from 0.5 to 1.5
- ln1_bias: float32 [768], P('seq'), may hold values from -1.75 to 1.75
- w_qkv: float32 [768, 2304], P('img', 'seq'), may hold values from -0.21875 to 0.21875
- b_qv: float32 [1536], P('seq'), may hold values from -3 to 3
- w_out: float32 [768, 768], P('img', 'seq'), may hold values from -0.625 to 0.625
- b_out: float32 [768], P('seq'), may hold values from -1.75 to 1.75
- ln2_gain: float32 [768], P('seq'), may hold values from 0.5 to 1.5
- ln2_bias: float32 [768], P('seq'), may hold values from -1.75 to 1.75
- w_up: float32 [768, 3072], P('img', 'seq'), may hold values from -0.21875 to 0.21875
- b_up: float32 [3072], P('seq'), may hold values from -3 to 3
- w_down: float32 [3072, 768], P('img', 'seq'), may hold values from -0.109375 to 0.109375
- b_down: float32 [768], P('seq'), may hold values from -1.75 to 1.75
- dy_big: bfloat16 [128, 200, 768], P(('img', 'seq')), may hold values from -6 to 6
- dy_small: bfloat16 [512, 40, 768], P(('img', 'seq')), may hold values from -6 to 6
Outputs:
- y_big: bfloat16 [128, 200, 768], P(('img', 'seq'))
- y_small: bfloat16 [512, 40, 768], P(('img', 'seq'))
- dx_big: bfloat16 [128, 200, 768], P(('img', 'seq'))
- dx_small: bfloat16 [512, 40, 768], P(('img', 'seq'))
- g_ln1_gain: float32 [768], P('seq')
- g_ln1_bias: float32 [768], P('seq')
- g_w_qkv: float32 [768, 2304], P('img', 'seq')
- g_b_qv: float32 [1536], P('seq')
- g_w_out: float32 [768, 768], P('img', 'seq')
- g_b_out: float32 [768], P('seq')
- g_ln2_gain: float32 [768], P('seq')
- g_ln2_bias: float32 [768], P('seq')
- g_w_up: float32 [768, 3072], P('img', 'seq')
- g_b_up: float32 [3072], P('seq')
- g_w_down: float32 [3072, 768], P('img', 'seq')
- g_b_down: float32 [768], P('seq')
Inputs may be any that keep to these rules, and one draw needn't show every extreme that they name: `mask_big`: each 224px crop's mask is 1 on its first 175 to 200 slots and 0 after; some crop has all slots valid and some the fewest. `mask_small`: each 96px crop's mask is 1 on its first 35 to 40 slots and 0 after; some crop has all slots valid and some the fewest.
All inputs are finite; a program needn't handle non-finite values.
Results may differ from a plain program's by a relative error of at most 0.014.
Values may be sent and summed in bfloat16 or wider, within the bound.
A program may use at most 192 MiB of HBM per device.

v0:
```python
import jax
import jax.numpy as jnp
from jax import lax
from jax.sharding import PartitionSpec as P

HEADS = 12
HEAD_DIM = 64


EPSILON = 1e-06
NEGATIVE = -1e30


def layer_norm(values, gain_vec, shift_vec):
    row_mean = jnp.mean(values, axis=-1, keepdims=True)
    centred = values - row_mean
    variance = jnp.mean(centred * centred, axis=-1, keepdims=True)
    return centred * lax.rsqrt(variance + EPSILON) * gain_vec + shift_vec


def gelu_exact(values):
    return jax.nn.gelu(values, approximate=False)


def head_scores(heads_in, key_valid, local_heads):
    crop_count, length = (heads_in.shape[0], heads_in.shape[1])
    pieces = heads_in.reshape(crop_count, length, 3, local_heads, HEAD_DIM)
    queries, key_rows, value_rows = (pieces[:, :, 0], pieces[:, :, 1], pieces[:, :, 2])
    raw_scores = jnp.einsum(
        "cqhd,ckhd->chqk", queries, key_rows, preferred_element_type=jnp.float32
    )
    scores = jnp.where(key_valid[:, None, None, :] > 0, raw_scores * HEAD_DIM ** (-0.5), NEGATIVE)
    return (queries, key_rows, value_rows, scores)


def attend(heads_in, key_valid, local_heads):
    crop_count, length = (heads_in.shape[0], heads_in.shape[1])
    queries, key_rows, value_rows, scores = head_scores(heads_in, key_valid, local_heads)
    row_max = jnp.max(scores, axis=-1, keepdims=True)
    exponent = jnp.exp(scores - row_max)
    row_total = jnp.sum(exponent, axis=-1, keepdims=True)
    softmax_w = (exponent / row_total).astype(jnp.bfloat16)
    mixed_out = jnp.einsum(
        "chqk,ckhd->cqhd", softmax_w, value_rows, preferred_element_type=jnp.float32
    )
    log_total = row_max + jnp.log(row_total)
    mixed_out = mixed_out.astype(jnp.bfloat16).reshape(
        crop_count, length, 1, local_heads * HEAD_DIM
    )
    return (mixed_out, log_total)


def attend_back(heads_in, key_valid, log_total, grad_heads, local_heads):
    crop_count, length = (heads_in.shape[0], heads_in.shape[1])
    queries, key_rows, value_rows, scores = head_scores(heads_in, key_valid, local_heads)
    softmax_f = jnp.exp(scores - log_total)
    grad_mixed = grad_heads.reshape(crop_count, length, local_heads, HEAD_DIM)
    grad_soft = jnp.einsum(
        "cqhd,ckhd->chqk", grad_mixed, value_rows, preferred_element_type=jnp.float32
    )
    inner_sum = jnp.sum(softmax_f * grad_soft, axis=-1, keepdims=True)
    grad_raw = (softmax_f * (grad_soft - inner_sum) * HEAD_DIM ** (-0.5)).astype(jnp.bfloat16)
    grad_query = jnp.einsum(
        "chqk,ckhd->cqhd", grad_raw, key_rows, preferred_element_type=jnp.float32
    )
    grad_key = jnp.einsum("chqk,cqhd->ckhd", grad_raw, queries, preferred_element_type=jnp.float32)
    grad_value = jnp.einsum(
        "chqk,cqhd->ckhd",
        softmax_f.astype(jnp.bfloat16),
        grad_mixed,
        preferred_element_type=jnp.float32,
    )
    stacked = jnp.stack([grad_query, grad_key, grad_value], axis=2).astype(jnp.bfloat16)
    return stacked.reshape(crop_count, length, 3, 1, local_heads * HEAD_DIM)


def body(
    x_big,
    x_small,
    mask_big,
    mask_small,
    ln1_gain,
    ln1_bias,
    w_qkv,
    b_qv,
    w_out,
    b_out,
    ln2_gain,
    ln2_bias,
    w_up,
    b_up,
    w_down,
    b_down,
    dy_big,
    dy_small,
):
    n_seq = lax.axis_size("seq")
    local_heads = HEADS // n_seq
    head_span = local_heads * HEAD_DIM
    model_width = x_big.shape[2]
    big_crops, big_length = (x_big.shape[0], x_big.shape[1])
    small_crops, small_length = (x_small.shape[0], x_small.shape[1])
    big_rows = big_crops * big_length
    sectioned = (
        lax.all_gather(w_qkv.astype(jnp.bfloat16), "seq", axis=1, tiled=True),
        lax.all_gather(w_out.astype(jnp.bfloat16), "seq", axis=1, tiled=True),
        lax.all_gather(w_up.astype(jnp.bfloat16), "seq", axis=1, tiled=True),
        lax.all_gather(w_down.astype(jnp.bfloat16), "seq", axis=1, tiled=True),
        lax.all_gather(ln1_gain.astype(jnp.bfloat16), "seq", axis=0, tiled=True),
        lax.all_gather(ln1_bias.astype(jnp.bfloat16), "seq", axis=0, tiled=True),
        lax.all_gather(b_qv.astype(jnp.bfloat16), "seq", axis=0, tiled=True),
        lax.all_gather(b_out.astype(jnp.bfloat16), "seq", axis=0, tiled=True),
        lax.all_gather(ln2_gain.astype(jnp.bfloat16), "seq", axis=0, tiled=True),
        lax.all_gather(ln2_bias.astype(jnp.bfloat16), "seq", axis=0, tiled=True),
        lax.all_gather(b_up.astype(jnp.bfloat16), "seq", axis=0, tiled=True),
        lax.all_gather(b_down.astype(jnp.bfloat16), "seq", axis=0, tiled=True),
    )
    whole_w = (
        lax.all_gather(sectioned[0], "img", axis=0, tiled=True),
        lax.all_gather(sectioned[1], "img", axis=0, tiled=True),
        lax.all_gather(sectioned[2], "img", axis=0, tiled=True),
        lax.all_gather(sectioned[3], "img", axis=0, tiled=True),
    )
    vectors = sectioned[4:]
    qkv_full, out_full, up_full, down_full = whole_w
    gain_one, shift_one, bias_qv, bias_out, gain_two, shift_two, bias_up, bias_down = tuple(
        (vec.astype(jnp.float32) for vec in vectors)
    )
    tokens = jnp.concatenate(
        [x_big.reshape(big_rows, model_width), x_small.reshape(-1, model_width)], axis=0
    ).astype(jnp.float32)
    normed_one, pull_one = jax.vjp(layer_norm, tokens, gain_one, shift_one)
    input_one = normed_one.astype(jnp.bfloat16)
    bias_qkv = jnp.concatenate(
        [bias_qv[:model_width], jnp.zeros((model_width,), jnp.float32), bias_qv[model_width:]]
    )
    projected = (
        jnp.dot(input_one, qkv_full, preferred_element_type=jnp.float32) + bias_qkv
    ).astype(jnp.bfloat16)
    split_big = projected[:big_rows].reshape(big_crops, big_length, 3, n_seq, head_span)
    split_small = projected[big_rows:].reshape(small_crops, small_length, 3, n_seq, head_span)
    heads_big, heads_small = (
        lax.all_to_all(split_big, "seq", split_axis=3, concat_axis=0, tiled=True),
        lax.all_to_all(split_small, "seq", split_axis=3, concat_axis=0, tiled=True),
    )
    mixed_big, total_big = attend(heads_big, mask_big, local_heads)
    mixed_small, total_small = attend(heads_small, mask_small, local_heads)
    back_big, back_small = (
        lax.all_to_all(mixed_big, "seq", split_axis=0, concat_axis=2, tiled=True),
        lax.all_to_all(mixed_small, "seq", split_axis=0, concat_axis=2, tiled=True),
    )
    mixed_tok = jnp.concatenate(
        [back_big.reshape(big_rows, model_width), back_small.reshape(-1, model_width)], axis=0
    )
    middle = tokens + jnp.dot(mixed_tok, out_full, preferred_element_type=jnp.float32) + bias_out
    normed_two, pull_two = jax.vjp(layer_norm, middle, gain_two, shift_two)
    input_two = normed_two.astype(jnp.bfloat16)
    up_proj = jnp.dot(input_two, up_full, preferred_element_type=jnp.float32) + bias_up
    activated_f, pull_act = jax.vjp(gelu_exact, up_proj)
    activated = activated_f.astype(jnp.bfloat16)
    result = middle + jnp.dot(activated, down_full, preferred_element_type=jnp.float32) + bias_down
    grad_out = jnp.concatenate(
        [dy_big.reshape(big_rows, model_width), dy_small.reshape(-1, model_width)], axis=0
    )
    grad_down = jnp.einsum("ti,tj->ij", activated, grad_out, preferred_element_type=jnp.float32)
    grad_bias_down = jnp.sum(grad_out.astype(jnp.float32), axis=0)
    grad_act = jnp.einsum("tj,ij->ti", grad_out, down_full, preferred_element_type=jnp.float32)
    (grad_up_f,) = pull_act(grad_act)
    grad_up_b = grad_up_f.astype(jnp.bfloat16)
    grad_upw = jnp.einsum("ti,tj->ij", input_two, grad_up_b, preferred_element_type=jnp.float32)
    grad_bias_up = jnp.sum(grad_up_b.astype(jnp.float32), axis=0)
    grad_in_two = jnp.einsum("tj,ij->ti", grad_up_b, up_full, preferred_element_type=jnp.float32)
    grad_middle_ln, grad_gain_two, grad_shift_two = pull_two(grad_in_two)
    grad_middle = grad_out.astype(jnp.float32) + grad_middle_ln
    grad_branch = grad_middle.astype(jnp.bfloat16)
    grad_bias_out = jnp.sum(grad_branch.astype(jnp.float32), axis=0)
    grad_outw = jnp.einsum("ti,tj->ij", mixed_tok, grad_branch, preferred_element_type=jnp.float32)
    grad_mixed = jnp.einsum(
        "tj,ij->ti", grad_branch, out_full, preferred_element_type=jnp.float32
    ).astype(jnp.bfloat16)
    grad_split_big = grad_mixed[:big_rows].reshape(big_crops, big_length, n_seq, head_span)
    grad_split_small = grad_mixed[big_rows:].reshape(small_crops, small_length, n_seq, head_span)
    grad_heads_big, grad_heads_small = (
        lax.all_to_all(grad_split_big, "seq", split_axis=2, concat_axis=0, tiled=True),
        lax.all_to_all(grad_split_small, "seq", split_axis=2, concat_axis=0, tiled=True),
    )
    grad_qkv_big = attend_back(heads_big, mask_big, total_big, grad_heads_big, local_heads)
    grad_qkv_small = attend_back(
        heads_small, mask_small, total_small, grad_heads_small, local_heads
    )
    grad_tok_big, grad_tok_small = (
        lax.all_to_all(grad_qkv_big, "seq", split_axis=0, concat_axis=3, tiled=True),
        lax.all_to_all(grad_qkv_small, "seq", split_axis=0, concat_axis=3, tiled=True),
    )
    grad_projected = jnp.concatenate(
        [
            grad_tok_big.reshape(big_rows, 3 * model_width),
            grad_tok_small.reshape(-1, 3 * model_width),
        ],
        axis=0,
    )
    grad_qkvw = jnp.einsum(
        "ti,tj->ij", input_one, grad_projected, preferred_element_type=jnp.float32
    )
    grad_proj_sums = jnp.sum(grad_projected.astype(jnp.float32), axis=0)
    grad_bias_qv = jnp.concatenate(
        [grad_proj_sums[:model_width], grad_proj_sums[2 * model_width :]]
    )
    grad_in_one = jnp.einsum(
        "tj,ij->ti", grad_projected, qkv_full, preferred_element_type=jnp.float32
    )
    grad_tokens_ln, grad_gain_one, grad_shift_one = pull_one(grad_in_one)
    grad_tokens = (grad_middle + grad_tokens_ln).astype(jnp.bfloat16)
    vector_sums = lax.psum(
        (
            grad_gain_one,
            grad_shift_one,
            grad_bias_qv,
            grad_bias_out,
            grad_gain_two,
            grad_shift_two,
            grad_bias_up,
            grad_bias_down,
        ),
        "img",
    )
    reduced = (
        lax.psum_scatter(grad_qkvw, "img", scatter_dimension=0, tiled=True),
        lax.psum_scatter(grad_outw, "img", scatter_dimension=0, tiled=True),
        lax.psum_scatter(grad_upw, "img", scatter_dimension=0, tiled=True),
        lax.psum_scatter(grad_down, "img", scatter_dimension=0, tiled=True),
    )
    finished = (
        lax.psum_scatter(
            reduced[0].astype(jnp.bfloat16), "seq", scatter_dimension=1, tiled=True
        ).astype(jnp.float32),
        lax.psum_scatter(
            reduced[1].astype(jnp.bfloat16), "seq", scatter_dimension=1, tiled=True
        ).astype(jnp.float32),
        lax.psum_scatter(
            reduced[2].astype(jnp.bfloat16), "seq", scatter_dimension=1, tiled=True
        ).astype(jnp.float32),
        lax.psum_scatter(
            reduced[3].astype(jnp.bfloat16), "seq", scatter_dimension=1, tiled=True
        ).astype(jnp.float32),
        lax.psum_scatter(
            vector_sums[0].astype(jnp.bfloat16), "seq", scatter_dimension=0, tiled=True
        ).astype(jnp.float32),
        lax.psum_scatter(
            vector_sums[1].astype(jnp.bfloat16), "seq", scatter_dimension=0, tiled=True
        ).astype(jnp.float32),
        lax.psum_scatter(
            vector_sums[2].astype(jnp.bfloat16), "seq", scatter_dimension=0, tiled=True
        ).astype(jnp.float32),
        lax.psum_scatter(
            vector_sums[3].astype(jnp.bfloat16), "seq", scatter_dimension=0, tiled=True
        ).astype(jnp.float32),
        lax.psum_scatter(
            vector_sums[4].astype(jnp.bfloat16), "seq", scatter_dimension=0, tiled=True
        ).astype(jnp.float32),
        lax.psum_scatter(
            vector_sums[5].astype(jnp.bfloat16), "seq", scatter_dimension=0, tiled=True
        ).astype(jnp.float32),
        lax.psum_scatter(
            vector_sums[6].astype(jnp.bfloat16), "seq", scatter_dimension=0, tiled=True
        ).astype(jnp.float32),
        lax.psum_scatter(
            vector_sums[7].astype(jnp.bfloat16), "seq", scatter_dimension=0, tiled=True
        ).astype(jnp.float32),
    )
    y_big = result[:big_rows].reshape(big_crops, big_length, model_width).astype(jnp.bfloat16)
    y_small = result[big_rows:].reshape(small_crops, small_length, model_width).astype(jnp.bfloat16)
    dx_big = grad_tokens[:big_rows].reshape(big_crops, big_length, model_width)
    dx_small = grad_tokens[big_rows:].reshape(small_crops, small_length, model_width)
    return (
        y_big,
        y_small,
        dx_big,
        dx_small,
        finished[4],
        finished[5],
        finished[0],
        finished[6],
        finished[1],
        finished[7],
        finished[8],
        finished[9],
        finished[2],
        finished[10],
        finished[3],
        finished[11],
    )


def solution(mesh):
    placed = (
        P(("img", "seq"), None, None),
        P(("img", "seq"), None, None),
        P("img", None),
        P("img", None),
        P("seq"),
        P("seq"),
        P("img", "seq"),
        P("seq"),
        P("img", "seq"),
        P("seq"),
        P("seq"),
        P("seq"),
        P("img", "seq"),
        P("seq"),
        P("img", "seq"),
        P("seq"),
        P(("img", "seq"), None, None),
        P(("img", "seq"), None, None),
    )
    return jax.shard_map(
        body,
        mesh=mesh,
        in_specs=placed,
        out_specs=(
            P(("img", "seq"), None, None),
            P(("img", "seq"), None, None),
            P(("img", "seq"), None, None),
            P(("img", "seq"), None, None),
            P("seq"),
            P("seq"),
            P("img", "seq"),
            P("seq"),
            P("img", "seq"),
            P("seq"),
            P("seq"),
            P("seq"),
            P("img", "seq"),
            P("seq"),
            P("img", "seq"),
            P("seq"),
        ),
        check_vma=False,
    )
```

profile of v0, /device:TPU:0, one launch (start us, length us, event | category | flops | bytes accessed | tf_op | source)
XLA Modules:
  0.0 1136.7 jit_solution(9841465774132675369)
XLA Ops:
  8.4 17.0 %all-gather = bf16[4,576,96]{1,2,0:T(8,128)(2,1)S(1)} all-gather(bf16[1,576,96]{1,2,0:T(8,128)(2,1)S(1)} %convert_bitcast_fusion.4), channel_id=1, replica_groups=mesh['img'=8,'seq'=4] {'seq'}, dimensions={0}, use_global_device_ids=true | all-gather | bytes 552960 | tf_op jit(solution)/shard_map/all_gather | solution.py:105
  33.9 19.5 %all-reduce.16 = (bf16[768]{0:T(1024)(128)(2,1)S(1)}, bf16[768]{0:T(1024)(128)(2,1)S(1)}, bf16[768]{0:T(1024)(128)(2,1)S(1)}, bf16[768]{0:T(1024)(128)(2,1)S(1)}, bf16[768]{0:T(1024)(128)(2,1)S(1)}) all-reduce(bf16[768]{0:T(1024)(128)(2,1)S(1)} %dynamic-update-slice.1, ...), channel_id=1, replica_groups=mesh['img'=8,'seq'=4] {'seq'}, use_global_device_ids=true, to_apply=%add.1 | all-reduce | flops 3840 | bytes 15360
  53.4 11.9 %all-gather.1 = bf16[4,1,384]{2,1,0:T(2,128)(2,1)S(1)} all-gather(bf16[1,1,384]{2,1,0:T(2,128)(2,1)S(1)} %reshape.338), channel_id=1, replica_groups=mesh['img'=8,'seq'=4] {'seq'}, dimensions={0}, use_global_device_ids=true | all-gather | bytes 3840 | tf_op jit(solution)/shard_map/all_gather | solution.py:111
  100.6 88.9 %all_gather.53 = bf16[96,768]{0,1:T(8,128)(2,1)S(1)} all-gather(bf16[96,192]{0,1:T(8,128)(2,1)S(1)} %copy.151), channel_id=1, replica_groups=mesh['img'=8,'seq'=4] {'seq'}, dimensions={1}, use_global_device_ids=true | all-gather | bytes 184320 | tf_op jit(solution)/shard_map/all_gather | solution.py:106
  220.1 113.6 %all_gather.58 = bf16[96,3072]{1,0:T(8,128)(2,1)} all-gather(bf16[96,768]{1,0:T(8,128)(2,1)S(1)} %convert_element_type.250), channel_id=1, replica_groups=mesh['img'=8,'seq'=4] {'seq'}, dimensions={1}, use_global_device_ids=true | all-gather | bytes 737280 | tf_op jit(solution)/shard_map/all_gather | solution.py:107
  333.9 15.1 %reshape.305 = bf16[64,40,3,3,64]{4,3,1,2,0:T(4,128)(2,1)} reshape(bf16[4,16,40,3,1,192]{5,2,3,1,0,4:T(8,128)(2,1)} %bitcast.18) | data formatting | bytes 5898240 | tf_op jit(solution)/shard_map/reshape | solution.py:27
  389.9 12.0 %all-to-all-done.3 = bf16[64,40,1,192]{3,1,2,0:T(8,128)(2,1)S(1)} async-done(((bf16[64,40,1,192]{3,1,2,0:T(8,128)(2,1)}), bf16[64,40,1,192]{3,1,2,0:T(8,128)(2,1)S(1)}, u32[]{:S(2)}, u32[]{:S(2)}) %all-to-all-start.3) | async-done | bytes 983072 | tf_op jit(solution)/shard_map/all_to_all | solution.py:150
  407.3 46.0 %all_gather.61 = bf16[384,768]{0,1:T(8,128)(2,1)} all-gather(bf16[384,192]{0,1:T(8,128)(2,1)S(1)} %convert_element_type.254), channel_id=1, replica_groups=mesh['img'=8,'seq'=4] {'seq'}, dimensions={1}, use_global_device_ids=true | all-gather | bytes 737280 | tf_op jit(solution)/shard_map/all_gather | solution.py:108
  453.4 13.0 %all-gather.2 = bf16[4,1,768]{2,1,0:T(2,128)(2,1)S(1)} all-gather(bf16[1,1,768]{2,1,0:T(2,128)(2,1)S(1)} %reshape.340), channel_id=1, replica_groups=mesh['img'=8,'seq'=4] {'seq'}, dimensions={0}, use_global_device_ids=true | all-gather | bytes 7680 | tf_op jit(solution)/shard_map/all_gather | solution.py:115
  490.4 52.0 %multiply_convert_fusion = (bf16[1440,3072]{1,0:T(8,128)(2,1)}, f32[1440,3072]{1,0:T(8,128)}, f32[1440,3072]{1,0:T(8,128)}) fusion(f32[3072]{0:T(1024)S(1)} %bitcast.201, bf16[768,3072]{1,0:T(8,128)(2,1)} %all-gather.12.cloned.1.call-done, f32[1440,768]{1,0:T(8,128)} %copy-done.3, f32[768]{0:T(1024)S(1)} %convert_element_type.248, ...), kind=kOutput, calls=%fused_computation.6 | convolution fusion | flops 7092264960 | bytes 53409024 | tf_op jit(solution)/shard_map/dot_general | solution.py:158
  542.5 23.2 %convert_reduce_fusion = (f32[3072]{0:T(1024)}, bf16[1440,3072]{1,0:T(8,128)(2,1)}) fusion(f32[1440,3072]{1,0:T(8,128)} %get-tuple-element.132, bf16[3072,768]{0,1:T(8,128)(2,1)} %all-gather.14.cloned.1.call-done, bf16[640,768]{1,0:T(8,128)(2,1)S(1)} %bitcast.184, bf16[800,768]{1,0:T(8,128)(2,1)S(1)} %bitcast.178, f32[1440,3072]{1,0:T(8,128)} %get-tuple-element.148, ...), kind=kOutput, calls=%fused_computation.4 | convolution fusion | flops 6874395648 | bytes 51191808 | tf_op jit(solution)/shard_map/tj,ij->ti/dot_general | solution.py:167
  565.7 13.1 %multiply_reduce_fusion.1 = (f32[768]{0:T(1024)S(1)}, f32[1440]{0:T(1024)S(1)}, f32[768]{0:T(1024)S(1)}, f32[1440,768]{1,0:T(8,128)S(1)}) fusion(f32[1440,768]{1,0:T(8,128)S(1)} %copy-done.4, f32[1440]{0:T(1024)S(1)} %fusion.100, f32[1440]{0:T(1024)S(1)} %broadcast_multiply_fusion, f32[768]{0:T(1024)S(1)} %convert_element_type.246, ...), kind=kOutput, calls=%fused_computation.70 | convolution fusion | flops 6803616768 | bytes 22439808 | tf_op jit(solution)/shard_map/tj,ij->ti/dot_general | solution.py:172
  588.2 42.6 %reduce-scatter.17.cloned.1.call-done = f32[96,768]{1,0:T(8,128)} async-done(((f32[768,768]{1,0:T(8,128)}), f32[96,768]{1,0:T(8,128)}) %reduce-scatter.17.cloned.1.call-update) | async-done | bytes 294928 | tf_op jit(solution)/shard_map/reduce_scatter | solution.py:229
  634.2 12.7 %fusion.119 = f32[3072,768]{1,0:T(8,128)} fusion(bf16[1440,3072]{1,0:T(8,128)(2,1)} %get-tuple-element.131, bf16[640,768]{1,0:T(8,128)(2,1)} %bitcast.182, bf16[800,768]{1,0:T(8,128)(2,1)S(1)} %bitcast.180), kind=kOutput, calls=%fused_computation.163 | convolution fusion | flops 6799196160 | bytes 20496384 | tf_op jit(solution)/shard_map/ti,tj->ij/dot_general | solution.py:165
  665.7 16.1 %fusion.124 = f32[768,3072]{1,0:T(8,128)} fusion(bf16[1440,3072]{1,0:T(8,128)(2,1)} %get-tuple-element.152, f32[1440,768]{1,0:T(8,128)} %copy-done.3, f32[768]{0:T(1024)S(1)} %convert_element_type.248, f32[768]{0:T(1024)S(1)} %convert_element_type.246, f32[1440]{0:T(1024)S(1)} %fusion.100, f32[1440]{0:T(1024)S(1)} %broadcast_multiply_fusion), kind=kOutput, calls=%fused_computation.166 | convolution fusion | flops 6800302080 | bytes 22725888 | tf_op jit(solution)/shard_map/ti,tj->ij/dot_general | solution.py:170
  772.3 18.4 %fusion.88 = bf16[16,3,64,200]{3,2,1,0:T(8,128)(2,1)S(1)} fusion(f32[16,3,200,200]{2,3,1,0:T(8,128)} %fusion.97, f32[16,3,200,200]{2,3,1,0:T(8,128)} %copy-done.11, f32[16,3,200]{2,1,0:T(4,128)S(1)} %log_add_fusion.1, pred[16,200]{1,0:T(8,128)(4,1)S(1)} %copy-done.46, bf16[16,200,3,3,64]{1,4,3,0,2:T(8,128)(2,1)} %bitcast.170), kind=kOutput, calls=%fused_computation.108 | convolution fusion | flops 267504192 | bytes 42262528 | tf_op jit(solution)/shard_map/chqk,ckhd->cqhd/dot_general | solution.py:63
  790.7 18.6 %fusion.91 = bf16[16,3,64,200]{3,2,1,0:T(8,128)(2,1)S(1)} fusion(f32[16,3,200,200]{2,3,1,0:T(8,128)} %fusion.97, f32[16,3,200,200]{2,3,1,0:T(8,128)} %copy-done.11, f32[16,3,200]{2,1,0:T(4,128)S(1)} %log_add_fusion.1, pred[16,200]{1,0:T(8,128)(4,1)S(1)} %copy-done.46, bf16[16,200,3,3,64]{1,4,3,0,2:T(8,128)(2,1)} %bitcast.171), kind=kOutput, calls=%fused_computation.109 | convolution fusion | flops 267504192 | bytes 42262528 | tf_op jit(solution)/shard_map/chqk,cqhd->ckhd/dot_general | solution.py:66
  818.9 32.8 %all-to-all-done.7 = bf16[64,40,3,1,192]{4,1,3,2,0:T(8,128)(2,1)} async-done(((bf16[64,40,3,1,192]{4,1,3,2,0:T(8,128)(2,1)}), bf16[64,40,3,1,192]{4,1,3,2,0:T(8,128)(2,1)}, u32[]{:S(2)}, u32[]{:S(2)}) %all-to-all-start.7) | async-done | bytes 2949152 | tf_op jit(solution)/shard_map/all_to_all | solution.py:193
  871.5 89.1 %all-to-all-done.5 = bf16[16,200,3,1,192]{1,4,3,2,0:T(8,128)(2,1)} async-done(((bf16[16,200,3,1,192]{1,4,3,2,0:T(8,128)(2,1)}), bf16[16,200,3,1,192]{1,4,3,2,0:T(8,128)(2,1)}, u32[]{:S(2)}, u32[]{:S(2)}) %all-to-all-start.5) | async-done | bytes 3686432 | tf_op jit(solution)/shard_map/all_to_all | solution.py:192
  997.9 12.8 %fusion.126 = (f32[768]{0:T(1024)S(1)}, f32[1440]{0:T(1024)S(1)}, f32[1440,768]{1,0:T(8,128)}) fusion(f32[768]{0:T(1024)S(1)} %copy-done.43, f32[1440]{0:T(1024)S(1)} %copy-done.34, bf16[640,768]{1,0:T(8,128)(2,1)S(1)} %bitcast.164, bf16[800,768]{1,0:T(8,128)(2,1)S(1)} %bitcast.156, bf16[1440,2304]{1,0:T(8,128)(2,1)} %copy-done.6, ...), kind=kOutput, calls=%fused_computation.168 | convolution fusion | flops 5106030080 | bytes 16827648 | tf_op jit(solution)/shard_map/tj,ij->ti/dot_general | solution.py:209
  1032.0 23.4 %all-reduce.14 = (bf16[768]{0:T(1024)(128)(2,1)S(1)}, bf16[768]{0:T(1024)(128)(2,1)S(1)}, bf16[1536]{0:T(1024)(128)(2,1)S(1)}, bf16[768]{0:T(1024)(128)(2,1)S(1)...) all-reduce(f32[768]{0:T(1024)S(1)} %get-tuple-element.98, ...), channel_id=1, replica_groups=mesh['img'=8,'seq'=4] {'img'}, use_global_device_ids=true, to_apply=%region_15.16 | all-reduce | flops 9216 | bytes 55296 | tf_op jit(solution)/shard_map/psum | solution.py:214
  1055.4 16.4 %all-reduce.15 = (bf16[768]{0:T(1024)(128)(2,1)S(1)}, bf16[768]{0:T(1024)(128)(2,1)S(1)}, bf16[768]{0:T(1024)(128)(2,1)S(1)}, bf16[1536]{0:T(1024)(128)(2,1)S(1)...) all-reduce(bf16[768]{0:T(1024)(128)(2,1)S(1)} %dynamic-update-slice, ...), channel_id=1, replica_groups=mesh['img'=8,'seq'=4] {'seq'}, use_global_device_ids=true, to_apply=%add.5 | all-reduce | flops 9984 | bytes 39936
  1074.2 12.9 %add_convert_fusion.2 = bf16[1440,768]{1,0:T(8,128)(2,1)S(1)} fusion(f32[1440,768]{1,0:T(8,128)} %copy-done.3, bf16[1440,3072]{1,0:T(8,128)(2,1)} %get-tuple-element.131, bf16[3072,768]{0,1:T(8,128)(2,1)} %all-gather.14.cloned.1.call-done, f32[768]{0:T(1024)S(1)} %convert_element_type.256), kind=kOutput, calls=%fused_computation.74 | convolution fusion | flops 6798090240 | bytes 20204544 | tf_op jit(solution)/shard_map/dot_general | solution.py:161
  1107.0 20.8 %reduce-scatter.25.cloned.1.call-done = bf16[576,96]{1,0:T(8,128)(2,1)} async-done(((bf16[2304,96]{1,0:T(8,128)(2,1)}), bf16[576,96]{1,0:T(8,128)(2,1)}) %reduce-scatter.25.cloned.1.call-update) | async-done | bytes 110608
  (294 shorter events, 376.7 us)
Async XLA Ops:
  7.2 60.2 %copy-start.8 = (bf16[16,40,768]{2,1,0:T(8,128)(2,1)S(1)}, bf16[16,40,768]{2,1,0:T(8,128)(2,1)}, u32[]{:S(2)}) copy-start(bf16[16,40,768]{2,1,0:T(8,128)(2,1)} %param.19) | copy-start | bytes 2949124
  7.2 61.6 %all-gather.8.cloned.1.call-start = ((), (), s32[]{:S(2)}) async-start(), calls=%async_computation.16 | async-start | bytes 3981312 | tf_op jit(solution)/shard_map/all_gather | solution.py:119
  95.5 119.1 %all-to-all-start.2 = ((bf16[16,40,3,4,192]{4,1,2,0,3:T(8,128)(2,1)}), bf16[16,40,3,4,192]{4,1,2,0,3:T(8,128)(2,1)}, u32[]{:S(2)}, u32[]{:S(2)}) async-start(bf16[16,40,3,4,192]{4,1,2,0,3:T(8,128)(2,1)} %copy.142), calls=%async_computation.2 | async-start | bytes 7864320 | tf_op jit(solution)/shard_map/all_to_all | solution.py:144
  100.5 382.3 %all-gather.10.cloned.1.call-start = ((), (), s32[]{:S(2)}) async-start(), calls=%async_computation.17 | async-start | bytes 1327104 | tf_op jit(solution)/shard_map/all_gather | solution.py:120
  214.6 119.1 %copy-start.44 = (s32[64,40]{0,1:T(8,128)S(1)}, s32[64,40]{0,1:T(8,128)}, u32[]{:S(2)}) copy-start(s32[64,40]{0,1:T(8,128)} %param.21) | copy-start | bytes 30724
  214.6 119.2 %copy-start.47 = (s32[16,200]{1,0:T(8,128)S(1)}, s32[16,200]{1,0:T(8,128)}, u32[]{:S(2)}) copy-start(s32[16,200]{1,0:T(8,128)} %param.20) | copy-start | bytes 38404
  214.7 155.6 %all-to-all-start = ((bf16[4,200,3,4,192]{1,4,2,0,3:T(8,128)(2,1)}), bf16[4,200,3,4,192]{1,4,2,0,3:T(8,128)(2,1)}, u32[]{:S(2)}, u32[]{:S(2)}) async-start(bf16[4,200,3,4,192]{1,4,2,0,3:T(8,128)(2,1)} %copy.137), calls=%async_computation | async-start | bytes 9437184 | tf_op jit(solution)/shard_map/all_to_all | solution.py:143
  220.0 270.4 %all-gather.12.cloned.1.call-start = ((), (), s32[]{:S(2)}) async-start(), calls=%async_computation.18 | async-start | bytes 5308416 | tf_op jit(solution)/shard_map/all_gather | solution.py:121
  370.2 31.7 %all-to-all-start.3 = ((bf16[64,40,1,192]{3,1,2,0:T(8,128)(2,1)}), bf16[64,40,1,192]{3,1,2,0:T(8,128)(2,1)S(1)}, u32[]{:S(2)}, u32[]{:S(2)}) async-start(bf16[64,40,1,192]{3,1,2,0:T(8,128)(2,1)} %copy.149), calls=%async_computation.3 | async-start | bytes 2621440 | tf_op jit(solution)/shard_map/all_to_all | solution.py:150
  389.9 63.5 %copy-start.49 = (f32[768]{0:T(1024)S(1)}, f32[768]{0:T(1024)}, u32[]{:S(2)}) copy-start(f32[768]{0:T(1024)} %param.31) | copy-start | bytes 9220
  401.9 70.2 %all-to-all-start.1 = ((bf16[16,200,1,192]{1,3,2,0:T(8,128)(2,1)}), bf16[16,200,1,192]{1,3,2,0:T(8,128)(2,1)}, u32[]{:S(2)}, u32[]{:S(2)}) async-start(bf16[16,200,1,192]{1,3,2,0:T(8,128)(2,1)} %bitcast.192), calls=%async_computation.1 | async-start | bytes 3145728 | tf_op jit(solution)/shard_map/all_to_all | solution.py:149
  406.3 136.2 %all-gather.14.cloned.1.call-start = ((), (), s32[]{:S(2)}) async-start(), calls=%async_computation.19 | async-start | bytes 5308416 | tf_op jit(solution)/shard_map/all_gather | solution.py:122
  453.3 177.5 %reduce-scatter.17.cloned.1.call-start = ((), (), s32[]{:S(2)}) async-start(), calls=%async_computation.21 | async-start | bytes 2654208 | tf_op jit(solution)/shard_map/reduce_scatter | solution.py:229
  588.2 408.2 %reduce-scatter.27.cloned.1.call-start = ((), (), s32[]{:S(2)}) async-start(), calls=%async_computation.26 | async-start | bytes 245760
  634.2 376.5 %reduce-scatter.23.cloned.1.call-start = ((), (), s32[]{:S(2)}) async-start(), calls=%async_computation.24 | async-start | bytes 10616832 | tf_op jit(solution)/shard_map/reduce_scatter | solution.py:231
  654.8 35.9 %all-to-all-start.6 = ((bf16[16,40,4,192]{3,1,0,2:T(8,128)(2,1)}), bf16[16,40,4,192]{3,1,0,2:T(8,128)(2,1)S(1)}, u32[]{:S(2)}, u32[]{:S(2)}) async-start(bf16[16,40,4,192]{3,1,0,2:T(8,128)(2,1)} %copy.161), calls=%async_computation.6 | async-start | bytes 2621440 | tf_op jit(solution)/shard_map/all_to_all | solution.py:185
  659.4 362.5 %reduce-scatter.19.cloned.1.call-start = ((), (), s32[]{:S(2)}) async-start(), calls=%async_computation.22 | async-start | bytes 10616832 | tf_op jit(solution)/shard_map/reduce_scatter | solution.py:230
  690.8 68.4 %all-to-all-start.4 = ((bf16[4,200,4,192]{1,3,0,2:T(8,128)(2,1)}), bf16[4,200,4,192]{1,3,0,2:T(8,128)(2,1)}, u32[]{:S(2)}, u32[]{:S(2)}) async-start(bf16[4,200,4,192]{1,3,0,2:T(8,128)(2,1)} %copy.153), calls=%async_computation.4 | async-start | bytes 3145728 | tf_op jit(solution)/shard_map/all_to_all | solution.py:184
  759.2 92.5 %all-to-all-start.7 = ((bf16[64,40,3,1,192]{4,1,3,2,0:T(8,128)(2,1)}), bf16[64,40,3,1,192]{4,1,3,2,0:T(8,128)(2,1)}, u32[]{:S(2)}, u32[]{:S(2)}) async-start(bf16[64,40,3,1,192]{4,1,3,2,0:T(8,128)(2,1)} %copy.168), calls=%async_computation.7 | async-start | bytes 7864320 | tf_op jit(solution)/shard_map/all_to_all | solution.py:193
  851.7 108.9 %all-to-all-start.5 = ((bf16[16,200,3,1,192]{1,4,3,2,0:T(8,128)(2,1)}), bf16[16,200,3,1,192]{1,4,3,2,0:T(8,128)(2,1)}, u32[]{:S(2)}, u32[]{:S(2)}) async-start(bf16[16,200,3,1,192]{1,4,3,2,0:T(8,128)(2,1)} %pad_maximum_fusion.1), calls=%async_computation.5 | async-start | bytes 9437184 | tf_op jit(solution)/shard_map/all_to_all | solution.py:192
  856.7 215.2 %reduce-scatter.15.cloned.1.call-start = ((), (), s32[]{:S(2)}) async-start(), calls=%async_computation.20 | async-start | bytes 7962624 | tf_op jit(solution)/shard_map/reduce_scatter | solution.py:228
  993.8 100.8 %reduce-scatter.29.cloned.1.call-start = ((), (), s32[]{:S(2)}) async-start(), calls=%async_computation.27 | async-start | bytes 737280
  1013.1 92.3 %reduce-scatter.21.cloned.1.call-start = ((), (), s32[]{:S(2)}) async-start(), calls=%async_computation.23 | async-start | bytes 737280 | tf_op jit(solution)/shard_map/reduce_scatter | solution.py:240
  1024.2 103.6 %reduce-scatter.25.cloned.1.call-start = ((), (), s32[]{:S(2)}) async-start(), calls=%async_computation.25 | async-start | bytes 737280
  (49 other events, 459.6 us)
Sparse Core Ops, SparseCore 0:
  26.9 35.7 all-gather.7
  190.5 23.4 all-gather.9
  333.8 38.9 all-gather.11
  453.4 39.8 all-gather.13
  588.3 42.4 reduce-scatter.16
  634.3 19.3 reduce-scatter.26
  657.2 74.6 reduce-scatter.22
  735.4 76.4 reduce-scatter.18
  994.0 64.4 reduce-scatter.14
  1060.7 21.8 reduce-scatter.28
  1085.1 20.2 reduce-scatter.20
  1107.6 20.2 reduce-scatter.24
where the time goes:
time: 1150 us; the launch traced here: 1140 us
  blocking collectives  350 us (30%)
  matrix products  265 us (23%)
  waiting for transfers between devices  215 us (19%)
  local copies, waits for them, and re-layouts  193 us (17%)
  other arithmetic  55.2 us (5%)
  starting transfers between devices  40.2 us (3%)
  between operations  18.1 us (2%)
    all_gather x1, blocking collectives, body(): lax.all_gather(w_up.astype(jnp.bfloat16), 'seq', axis=1, tiled=True)  114 us
    all_to_all x1, waiting for transfers between devices, body(): lax.all_to_all(grad_qkv_big, 'seq', split_axis=0, concat_axis=3, tiled=True)  89.1 us
    all_gather x1, blocking collectives, body(): lax.all_gather(w_out.astype(jnp.bfloat16), 'seq', axis=1, tiled=True)  88.9 us
    dot_general x1, matrix products, body(): jnp.dot(input_two, up_full, preferred_element_type=jnp.float32) + bias_up  52 us
    all_gather x1, blocking collectives, body(): lax.all_gather(w_down.astype(jnp.bfloat16), 'seq', axis=1, tiled=True)  46 us
    reduce_scatter x1, waiting for transfers between devices, body(): lax.psum_scatter(grad_outw, 'img', scatter_dimension=0, tiled=True)  42.6 us
    unnamed x2, blocking collectives  35.9 us
    all_to_all x1, waiting for transfers between devices, body(): lax.all_to_all(grad_qkv_small, 'seq', split_axis=0, concat_axis=3, tiled=...  32.8 us
  transfers between devices with their start and end apart: 20, of which 7 were waited for; matrix products, arithmetic and copies ran while one was open for 37% of the time, Pallas kernels for 0%

commit v1 on v0

v1 whole, which is shorter than its diff:
```python
import jax
import jax.numpy as jnp
from jax import lax
from jax.sharding import PartitionSpec as P

HEADS = 12
HEAD_DIM = 64
AXES = ("img", "seq")

EPSILON = 1e-06
NEGATIVE = -1e30


def layer_norm(values, gain_vec, shift_vec):
    row_mean = jnp.mean(values, axis=-1, keepdims=True)
    centred = values - row_mean
    variance = jnp.mean(centred * centred, axis=-1, keepdims=True)
    return centred * lax.rsqrt(variance + EPSILON) * gain_vec + shift_vec


def gelu_exact(values):
    return jax.nn.gelu(values, approximate=False)


def head_scores(heads_in, key_valid):
    crop_count, length = (heads_in.shape[0], heads_in.shape[1])
    pieces = heads_in.reshape(crop_count, length, 3, HEADS, HEAD_DIM)
    queries, key_rows, value_rows = (pieces[:, :, 0], pieces[:, :, 1], pieces[:, :, 2])
    raw_scores = jnp.einsum(
        "cqhd,ckhd->chqk", queries, key_rows, preferred_element_type=jnp.float32
    )
    scores = jnp.where(key_valid[:, None, None, :] > 0, raw_scores * HEAD_DIM ** (-0.5), NEGATIVE)
    return (queries, key_rows, value_rows, scores)


def attend(heads_in, key_valid):
    crop_count, length = (heads_in.shape[0], heads_in.shape[1])
    queries, key_rows, value_rows, scores = head_scores(heads_in, key_valid)
    row_max = jnp.max(scores, axis=-1, keepdims=True)
    exponent = jnp.exp(scores - row_max)
    row_total = jnp.sum(exponent, axis=-1, keepdims=True)
    softmax_w = (exponent / row_total).astype(jnp.bfloat16)
    mixed_out = jnp.einsum(
        "chqk,ckhd->cqhd", softmax_w, value_rows, preferred_element_type=jnp.float32
    )
    log_total = row_max + jnp.log(row_total)
    return (mixed_out.astype(jnp.bfloat16).reshape(crop_count * length, -1), log_total)


def attend_back(heads_in, key_valid, log_total, grad_heads):
    crop_count, length = (heads_in.shape[0], heads_in.shape[1])
    queries, key_rows, value_rows, scores = head_scores(heads_in, key_valid)
    softmax_f = jnp.exp(scores - log_total)
    grad_mixed = grad_heads.reshape(crop_count, length, HEADS, HEAD_DIM)
    grad_soft = jnp.einsum(
        "cqhd,ckhd->chqk", grad_mixed, value_rows, preferred_element_type=jnp.float32
    )
    inner_sum = jnp.sum(softmax_f * grad_soft, axis=-1, keepdims=True)
    grad_raw = (softmax_f * (grad_soft - inner_sum) * HEAD_DIM ** (-0.5)).astype(jnp.bfloat16)
    grad_query = jnp.einsum(
        "chqk,ckhd->cqhd", grad_raw, key_rows, preferred_element_type=jnp.float32
    )
    grad_key = jnp.einsum("chqk,cqhd->ckhd", grad_raw, queries, preferred_element_type=jnp.float32)
    grad_value = jnp.einsum(
        "chqk,cqhd->ckhd",
        softmax_f.astype(jnp.bfloat16),
        grad_mixed,
        preferred_element_type=jnp.float32,
    )
    stacked = jnp.stack([grad_query, grad_key, grad_value], axis=2).astype(jnp.bfloat16)
    return stacked.reshape(crop_count * length, -1)


def gather_mats(mats):
    n_img, n_seq = lax.axis_size("img"), lax.axis_size("seq")
    flat = jnp.concatenate([m.astype(jnp.bfloat16).reshape(-1, 64) for m in mats], axis=0)
    whole = lax.all_gather(flat, AXES, axis=0, tiled=False)
    outs, at = [], 0
    for m in mats:
        rows = m.size // 64
        piece = whole[:, at : at + rows].reshape((n_img, n_seq) + m.shape)
        at += rows
        if m.ndim == 2:
            piece = piece.transpose(0, 2, 1, 3).reshape(n_img * m.shape[0], n_seq * m.shape[1])
        else:
            piece = piece[0].reshape(-1)
        outs.append(piece)
    return outs


def scatter_mats(mats):
    n_img, n_seq = lax.axis_size("img"), lax.axis_size("seq")
    blocks = []
    for m in mats:
        rows, cols = m.shape[0] // n_img, m.shape[1] // n_seq
        b = m.astype(jnp.bfloat16).reshape(n_img, rows, n_seq, cols).transpose(0, 2, 1, 3)
        blocks.append(b.reshape(n_img * n_seq, -1, 128))
    flat = jnp.concatenate(blocks, axis=1)
    mine = lax.psum_scatter(flat, AXES, scatter_dimension=0, tiled=False)
    outs, at = [], 0
    for m, b in zip(mats, blocks):
        piece = mine[at : at + b.shape[1]]
        at += b.shape[1]
        outs.append(piece.reshape(m.shape[0] // n_img, m.shape[1] // n_seq).astype(jnp.float32))
    return outs


def body(
    x_big,
    x_small,
    mask_big,
    mask_small,
    ln1_gain,
    ln1_bias,
    w_qkv,
    b_qv,
    w_out,
    b_out,
    ln2_gain,
    ln2_bias,
    w_up,
    b_up,
    w_down,
    b_down,
    dy_big,
    dy_small,
):
    n_seq = lax.axis_size("seq")
    where = lax.axis_index("seq")
    model_width = x_big.shape[2]
    big_crops, big_length = (x_big.shape[0], x_big.shape[1])
    small_crops, small_length = (x_small.shape[0], x_small.shape[1])
    big_rows = big_crops * big_length
    mask_big = lax.dynamic_slice_in_dim(mask_big, where * big_crops, big_crops, 0)
    mask_small = lax.dynamic_slice_in_dim(mask_small, where * small_crops, small_crops, 0)
    (
        qkv_full,
        gain_one,
        shift_one,
        bias_qv,
        bias_out,
        gain_two,
        shift_two,
        bias_up,
        bias_down,
    ) = gather_mats([w_qkv, ln1_gain, ln1_bias, b_qv, b_out, ln2_gain, ln2_bias, b_up, b_down])
    out_full, up_full, down_full = gather_mats([w_out, w_up, w_down])
    gain_one, shift_one, bias_qv, bias_out, gain_two, shift_two, bias_up, bias_down = tuple(
        (
            vec.astype(jnp.float32)
            for vec in (
                gain_one,
                shift_one,
                bias_qv,
                bias_out,
                gain_two,
                shift_two,
                bias_up,
                bias_down,
            )
        )
    )
    tokens = jnp.concatenate(
        [x_big.reshape(big_rows, model_width), x_small.reshape(-1, model_width)], axis=0
    ).astype(jnp.float32)
    normed_one, pull_one = jax.vjp(layer_norm, tokens, gain_one, shift_one)
    input_one = normed_one.astype(jnp.bfloat16)
    bias_qkv = jnp.concatenate(
        [bias_qv[:model_width], jnp.zeros((model_width,), jnp.float32), bias_qv[model_width:]]
    )
    projected = (
        jnp.dot(input_one, qkv_full, preferred_element_type=jnp.float32) + bias_qkv
    ).astype(jnp.bfloat16)
    heads_big = projected[:big_rows].reshape(big_crops, big_length, -1)
    heads_small = projected[big_rows:].reshape(small_crops, small_length, -1)
    mixed_big, total_big = attend(heads_big, mask_big)
    mixed_small, total_small = attend(heads_small, mask_small)
    mixed_tok = jnp.concatenate([mixed_big, mixed_small], axis=0)
    middle = tokens + jnp.dot(mixed_tok, out_full, preferred_element_type=jnp.float32) + bias_out
    normed_two, pull_two = jax.vjp(layer_norm, middle, gain_two, shift_two)
    input_two = normed_two.astype(jnp.bfloat16)
    up_proj = jnp.dot(input_two, up_full, preferred_element_type=jnp.float32) + bias_up
    activated_f, pull_act = jax.vjp(gelu_exact, up_proj)
    activated = activated_f.astype(jnp.bfloat16)
    result = middle + jnp.dot(activated, down_full, preferred_element_type=jnp.float32) + bias_down
    grad_out = jnp.concatenate(
        [dy_big.reshape(big_rows, model_width), dy_small.reshape(-1, model_width)], axis=0
    )
    grad_down = jnp.einsum("ti,tj->ij", activated, grad_out, preferred_element_type=jnp.float32)
    grad_bias_down = jnp.sum(grad_out.astype(jnp.float32), axis=0)
    grad_act = jnp.einsum("tj,ij->ti", grad_out, down_full, preferred_element_type=jnp.float32)
    (grad_up_f,) = pull_act(grad_act)
    grad_up_b = grad_up_f.astype(jnp.bfloat16)
    grad_upw = jnp.einsum("ti,tj->ij", input_two, grad_up_b, preferred_element_type=jnp.float32)
    grad_bias_up = jnp.sum(grad_up_b.astype(jnp.float32), axis=0)
    grad_in_two = jnp.einsum("tj,ij->ti", grad_up_b, up_full, preferred_element_type=jnp.float32)
    grad_middle_ln, grad_gain_two, grad_shift_two = pull_two(grad_in_two)
    grad_middle = grad_out.astype(jnp.float32) + grad_middle_ln
    grad_branch = grad_middle.astype(jnp.bfloat16)
    grad_bias_out = jnp.sum(grad_branch.astype(jnp.float32), axis=0)
    grad_outw = jnp.einsum("ti,tj->ij", mixed_tok, grad_branch, preferred_element_type=jnp.float32)
    grad_mixed = jnp.einsum(
        "tj,ij->ti", grad_branch, out_full, preferred_element_type=jnp.float32
    ).astype(jnp.bfloat16)
    grad_projected = jnp.concatenate(
        [
            attend_back(heads_big, mask_big, total_big, grad_mixed[:big_rows]),
            attend_back(heads_small, mask_small, total_small, grad_mixed[big_rows:]),
        ],
        axis=0,
    )
    grad_qkvw = jnp.einsum(
        "ti,tj->ij", input_one, grad_projected, preferred_element_type=jnp.float32
    )
    grad_proj_sums = jnp.sum(grad_projected.astype(jnp.float32), axis=0)
    grad_bias_qv = jnp.concatenate(
        [grad_proj_sums[:model_width], grad_proj_sums[2 * model_width :]]
    )
    grad_in_one = jnp.einsum(
        "tj,ij->ti", grad_projected, qkv_full, preferred_element_type=jnp.float32
    )
    grad_tokens_ln, grad_gain_one, grad_shift_one = pull_one(grad_in_one)
    grad_tokens = (grad_middle + grad_tokens_ln).astype(jnp.bfloat16)
    vectors = (
        grad_gain_one,
        grad_shift_one,
        grad_bias_qv,
        grad_bias_out,
        grad_gain_two,
        grad_shift_two,
        grad_bias_up,
        grad_bias_down,
    )
    vector_sums = lax.psum(jnp.concatenate(vectors), AXES)
    vec_out, at = [], 0
    for v in vectors:
        width = v.shape[0] // n_seq
        vec_out.append(lax.dynamic_slice(vector_sums, (at + where * width,), (width,)))
        at += v.shape[0]
    g_up, g_down = scatter_mats([grad_upw, grad_down])
    g_qkv, g_out = scatter_mats([grad_qkvw, grad_outw])
    y_big = result[:big_rows].reshape(big_crops, big_length, model_width).astype(jnp.bfloat16)
    y_small = result[big_rows:].reshape(small_crops, small_length, model_width).astype(jnp.bfloat16)
    dx_big = grad_tokens[:big_rows].reshape(big_crops, big_length, model_width)
    dx_small = grad_tokens[big_rows:].reshape(small_crops, small_length, model_width)
    return (
        y_big,
        y_small,
        dx_big,
        dx_small,
        vec_out[0],
        vec_out[1],
        g_qkv,
        vec_out[2],
        g_out,
        vec_out[3],
        vec_out[4],
        vec_out[5],
        g_up,
        vec_out[6],
        g_down,
        vec_out[7],
    )


def solution(mesh):
    rows3 = P(AXES, None, None)
    placed = (
        rows3,
        rows3,
        P("img", None),
        P("img", None),
        P("seq"),
        P("seq"),
        P("img", "seq"),
        P("seq"),
        P("img", "seq"),
        P("seq"),
        P("seq"),
        P("seq"),
        P("img", "seq"),
        P("seq"),
        P("img", "seq"),
        P("seq"),
        rows3,
        rows3,
    )
    return jax.shard_map(
        body,
        mesh=mesh,
        in_specs=placed,
        out_specs=(rows3,) * 4
        + (
            P("seq"),
            P("seq"),
            P("img", "seq"),
            P("seq"),
            P("img", "seq"),
            P("seq"),
            P("seq"),
            P("seq"),
            P("img", "seq"),
            P("seq"),
            P("img", "seq"),
            P("seq"),
        ),
        check_vma=False,
    )
```

time: 1150 us -> 880 us (0.77)
  blocking collectives: 350 us -> 39.8 us
  local copies, waits for them, and re-layouts: 193 us -> 376 us
  waiting for transfers between devices: 215 us -> 122 us
  starting transfers between devices: 40.2 us -> 0.16 us
    all_gather x6 -> x0, blocking collectives: 290 us -> none  [the longest x1 114 us: body(): lax.all_gather(w_up.astype(jnp.bfloat16), 'seq', axis=1, tiled=True)]
    all_to_all x8 -> x0, waiting for transfers between devices: 143 us -> none  [the longest x1 89.1 us: body(): lax.all_to_all(grad_qkv_big, 'seq', split_axis=0, concat_axis=3, tiled=True)]
    reshape x15 -> x34, local copies, waits for them, and re-layouts: 89.7 us -> 150 us  [the longest x4 44.4 us: gather_mats(): piece = whole[:, at:at + rows].reshape((n_img, n_seq) + m.shape)]
    all_gather x4 -> x2, waiting for transfers between devices: 0.02 us -> 55.9 us  [gather_mats(): whole = lax.all_gather(flat, AXES, axis=0, tiled=False)]
    slice x5 -> x11, local copies, waits for them, and re-layouts: 7.21 us -> 58.6 us  [the longest x7 52.6 us: gather_mats(): piece = whole[:, at:at + rows].reshape((n_img, n_seq) + m.shape)]
    convert_element_type x1 -> x24, local copies, waits for them, and re-layouts: 4.2 us -> 50.4 us  [the longest x3 36.6 us: attend_back(): jnp.stack([grad_query, grad_key, grad_value], axis=2).astype(jnp.bfloat16)]
    all_to_all x8 -> x0, starting transfers between devices: 39.4 us -> none  [the longest x1 5.9 us: body(): lax.all_to_all(grad_qkv_small, 'seq', split_axis=0, concat_axis=3, tiled=...]
    unnamed x2 -> x0, blocking collectives: 35.9 us -> none
  transfers between devices with their start and end apart: 20 -> 4, of which waited for: 7 -> 2; matrix products, arithmetic and copies ran while one was open for 37% -> 33% of each run, Pallas kernels for 0% -> 0%
where the time goes in v1:
time: 880 us; the launch traced here: 871 us
  local copies, waits for them, and re-layouts  376 us (43%)
  matrix products  256 us (29%)
  waiting for transfers between devices  122 us (14%)
  other arithmetic  62.1 us (7%)
  blocking collectives  39.8 us (5%)
  between operations  14.9 us (2%)
    reduce_scatter x2, waiting for transfers between devices, scatter_mats(): mine = lax.psum_scatter(flat, AXES, scatter_dimension=0, tiled=False)  66.3 us
    all_gather x2, waiting for transfers between devices, gather_mats(): whole = lax.all_gather(flat, AXES, axis=0, tiled=False)  55.9 us
    slice x7, local copies, waits for them, and re-layouts, gather_mats(): piece = whole[:, at:at + rows].reshape((n_img, n_seq) + m.shape)  52.6 us
    dot_general x1, matrix products, body(): jnp.dot(input_two, up_full, preferred_element_type=jnp.float32) + bias_up  48.1 us
    reshape x4, local copies, waits for them, and re-layouts, gather_mats(): piece = whole[:, at:at + rows].reshape((n_img, n_seq) + m.shape)  44.4 us
    psum x1, blocking collectives, body(): vector_sums = lax.psum(jnp.concatenate(vectors), AXES)  39.8 us
    unnamed x144, local copies, waits for them, and re-layouts  36.7 us
    convert_element_type x3, local copies, waits for them, and re-layouts, attend_back(): jnp.stack([grad_query, grad_key, grad_value], axis=2).astype(jnp.bfloat16)  36.6 us
  transfers between devices with their start and end apart: 4, of which 2 were waited for; matrix products, arithmetic and copies ran while one was open for 33% of the time, Pallas kernels for 0%

profile of v1, /device:TPU:0, one launch (start us, length us, event | category | flops | bytes accessed | tf_op | source)
XLA Modules:
  0.0 870.6 jit_solution(1051177203787296150)
XLA Ops:
  25.0 55.9 %all-gather.7.cloned.1.call-done = bf16[32,900,64]{1,2,0:T(8,128)(2,1)} async-done(((bf16[1,900,64]{1,2,0:T(8,128)(2,1)}), bf16[32,900,64]{1,2,0:T(8,128)(2,1)}) %all-gather.7.cloned.1.call-update) | async-done | bytes 3686416 | tf_op jit(solution)/shard_map/all_gather | solution.py:77
  97.2 10.8 %reshape.350 = bf16[8,4,96,576]{3,2,1,0:T(8,128)(2,1)} reshape(bf16[32,864,64]{2,1,0:T(8,128)(2,1)} %copy.143) | data formatting | bytes 7077888 | tf_op jit(solution)/shard_map/reshape | solution.py:81
  136.7 9.8 %reshape_reshape.9 = bf16[16,40,3,12,64]{4,3,2,1,0:T(8,128)(2,1)} reshape(bf16[640,2304]{1,0:T(8,128)(2,1)} %slice.190) | data formatting | bytes 5898240 | tf_op jit(solution)/shard_map/reshape;reshape | solution.py:27
  168.5 12.1 %reshape.398 = bf16[4,200,3,12,64]{4,3,2,1,0:T(8,128)(2,1)} reshape(bf16[800,2304]{1,0:T(8,128)(2,1)} %slice.186) | data formatting | bytes 7372800 | tf_op jit(solution)/shard_map/reshape;reshape | solution.py:27
  239.9 14.1 %fusion.135 = (bf16[32,1152,64]{1,2,0:T(8,128)(2,1)}, bf16[32,1152,64]{1,2,0:T(8,128)(2,1)}) fusion(bf16[32,2592,64]{1,2,0:T(8,128)(2,1)} %all-gather.9.cloned.1.call-done), kind=kLoop, calls=%fused_computation.187 | loop fusion | bytes 18874368 | tf_op jit(solution)/shard_map/slice | solution.py:81
  263.7 15.5 %reshape.361 = bf16[8,4,384,192]{3,2,1,0:T(8,128)(2,1)} reshape(bf16[32,1152,64]{2,1,0:T(8,128)(2,1)} %copy.174) | data formatting | bytes 9437184 | tf_op jit(solution)/shard_map/reshape | solution.py:81
  303.3 13.4 %reshape.359 = bf16[8,4,96,768]{3,2,1,0:T(8,128)(2,1)} reshape(bf16[32,1152,64]{2,1,0:T(8,128)(2,1)} %copy.170) | data formatting | bytes 9437184 | tf_op jit(solution)/shard_map/reshape | solution.py:81
  328.1 48.1 %multiply_convert_fusion = (bf16[1440,3072]{1,0:T(8,128)(2,1)}, f32[1440,3072]{1,0:T(8,128)}, f32[1440,3072]{1,0:T(8,128)}) fusion(f32[3072]{0:T(1024)S(1)} %reshape.382, bf16[768,3072]{1,0:T(8,128)(2,1)S(1)} %bitcast.185, f32[1440,768]{1,0:T(8,128)S(1)} %get-tuple-element.108, f32[768]{0:T(1024)S(1)} %reshape.381, f32[768]{0:T(1024)S(1)} %reshape.380, ...), kind=kOutput, calls=%fused_computation.6 | convolution fusion | flops 7092264960 | bytes 53409024 | tf_op jit(solution)/shard_map/dot_general | solution.py:182
  376.3 21.3 %convert_reduce_fusion = (f32[3072]{0:T(1024)}, bf16[1440,3072]{1,0:T(8,128)(2,1)}) fusion(f32[1440,3072]{1,0:T(8,128)} %get-tuple-element.76, bf16[3072,768]{0,1:T(8,128)(2,1)S(1)} %bitcast.184, bf16[640,768]{1,0:T(8,128)(2,1)} %bitcast.187, bf16[800,768]{1,0:T(8,128)(2,1)S(1)} %bitcast.177, f32[1440,3072]{1,0:T(8,128)} %get-tuple-element.109, ...), kind=kOutput, calls=%fused_computation.4 | convolution fusion | flops 6874395648 | bytes 51191808 | tf_op jit(solution)/shard_map/tj,ij->ti/dot_general | solution.py:191
  397.6 13.7 %multiply_reduce_fusion.1 = (f32[768]{0:T(1024)}, f32[1440]{0:T(1024)S(1)}, f32[768]{0:T(1024)}, f32[1440,768]{1,0:T(8,128)S(1)}) fusion(f32[1440,768]{1,0:T(8,128)S(1)} %get-tuple-element.108, f32[1440]{0:T(1024)S(1)} %fusion.104, f32[1440]{0:T(1024)S(1)} %broadcast_multiply_fusion, f32[768]{0:T(1024)S(1)} %reshape.380, ...), kind=kOutput, calls=%fused_computation.67 | convolution fusion | flops 6803616768 | bytes 22439808 | tf_op jit(solution)/shard_map/tj,ij->ti/dot_general | solution.py:196
  434.6 10.0 %convert_bitcast_fusion.2 = bf16[16,40,1,12,64]{4,1,3,0,2:T(8,128)(2,1)} fusion(f32[16,12,40,40]{2,3,1,0:T(8,128)} %fusion.100, f32[16,12,40,40]{2,3,1,0:T(8,128)} %copy-done.8, f32[16,12,40]{2,1,0:T(8,128)S(1)} %copy-done.35, bf16[16,40,1,12,64]{4,3,2,1,0:T(8,128)(2,1)} %copy-done.26), kind=kOutput, calls=%fused_computation.98 | convolution fusion | flops 41971240 | bytes 4454400 | tf_op jit(solution)/shard_map/chqk,ckhd->cqhd/dot_general | solution.py:60
  475.5 19.7 %fusion.92 = bf16[4,200,1,12,64]{1,4,3,0,2:T(8,128)(2,1)} fusion(f32[4,12,200,200]{2,3,1,0:T(8,128)} %fusion.81, f32[4,12,200]{2,1,0:T(8,128)S(1)} %copy-done.46, f32[4,12,200,200]{2,3,1,0:T(8,128)} %copy-done.3, pred[4,200]{1,0:T(4,128)(4,1)S(1)} %copy-done.52, bf16[4,200,1,12,64]{1,4,3,0,2:T(8,128)(2,1)S(1)} %copy-done.17), kind=kOutput, calls=%fused_computation.122 | convolution fusion | flops 267504192 | bytes 17856800 | tf_op jit(solution)/shard_map/chqk,ckhd->cqhd/dot_general | solution.py:60
  495.2 19.0 %fusion.87 = bf16[4,200,1,12,64]{1,4,3,0,2:T(8,128)(2,1)} fusion(f32[4,12,200,200]{2,3,1,0:T(8,128)} %fusion.81, f32[4,12,200]{2,1,0:T(8,128)S(1)} %copy-done.46, f32[4,12,200,200]{2,3,1,0:T(8,128)} %copy-done.3, pred[4,200]{1,0:T(4,128)(4,1)S(1)} %copy-done.52, bf16[4,200,1,12,64]{1,4,3,0,2:T(8,128)(2,1)S(1)} %copy-done.15), kind=kOutput, calls=%fused_computation.121 | convolution fusion | flops 267504192 | bytes 17856800 | tf_op jit(solution)/shard_map/chqk,cqhd->ckhd/dot_general | solution.py:63
  528.6 12.8 %copy.203 = bf16[16,40,3,12,64]{1,0,4,3,2:T(8,128)(2,1)} copy(bf16[16,40,3,12,64]{4,1,3,0,2:T(8,128)(2,1)} %pad_maximum_fusion.2) | data formatting | bytes 5898240 | tf_op jit(solution)/shard_map/convert_element_type | solution.py:70
  541.3 14.1 %reshape.397 = bf16[640,2304]{0,1:T(8,128)(2,1)} reshape(bf16[16,40,3,12,64]{1,0,4,3,2:T(8,128)(2,1)} %copy.203) | data formatting | bytes 5898240 | tf_op jit(solution)/shard_map/convert_element_type | solution.py:70
  574.5 12.6 %convolution_convert_fusion = bf16[768,2304]{1,0:T(8,128)(2,1)} fusion(bf16[640,2304]{0,1:T(8,128)(2,1)} %reshape.397, bf16[800,2304]{0,1:T(8,128)(2,1)} %convert_element_type.280, f32[768]{0:T(1024)S(1)} %copy-done.54, f32[768]{0:T(1024)S(1)} %copy-done.48, f32[1440]{0:T(1024)S(1)} %copy-done.39, f32[1440]{0:T(1024)S(1)} %copy-done.37, ...), kind=kOutput, calls=%fused_computation.48 | convolution fusion | flops 5121073152 | bytes 12403968 | tf_op jit(solution)/shard_map/ti,tj->ij/dot_general | solution.py:212
  614.8 12.5 %convolution_convert_fusion.1 = bf16[3072,768]{1,0:T(8,128)(2,1)} fusion(bf16[1440,3072]{1,0:T(8,128)(2,1)} %get-tuple-element.75, bf16[640,768]{1,0:T(8,128)(2,1)} %bitcast.188, bf16[800,768]{1,0:T(8,128)(2,1)S(1)} %bitcast.179), kind=kOutput, calls=%fused_computation.49 | convolution fusion | flops 6801555456 | bytes 15777792 | tf_op jit(solution)/shard_map/ti,tj->ij/dot_general | solution.py:189
  639.7 14.1 %convolution_convert_fusion.2 = bf16[768,3072]{1,0:T(8,128)(2,1)} fusion(bf16[1440,3072]{1,0:T(8,128)(2,1)} %get-tuple-element.113, f32[1440,768]{1,0:T(8,128)} %copy-done.6, f32[768]{0:T(1024)S(1)} %copy-done.56, f32[768]{0:T(1024)S(1)} %reshape.380, f32[1440]{0:T(1024)S(1)} %fusion.104, f32[1440]{0:T(1024)S(1)} %broadcast_multiply_fusion), kind=kOutput, calls=%fused_computation.50 | convolution fusion | flops 6802661376 | bytes 18007296 | tf_op jit(solution)/shard_map/ti,tj->ij/dot_general | solution.py:194
  653.8 9.8 %reshape.373 = bf16[8,96,4,768]{3,2,1,0:T(4,128)(2,1)} reshape(bf16[768,3072]{1,0:T(8,128)(2,1)} %convolution_convert_fusion.2) | data formatting | bytes 9437184 | tf_op jit(solution)/shard_map/reshape | solution.py:96
  687.6 12.0 %reshape.376 = bf16[32,576,128]{2,1,0:T(8,128)(2,1)} reshape(bf16[8,4,384,192]{3,2,1,0:T(8,128)(2,1)} %copy.194) | data formatting | bytes 9437184 | tf_op jit(solution)/shard_map/reshape | solution.py:97
  708.4 13.1 %add_convert_fusion.2 = bf16[1440,768]{1,0:T(8,128)(2,1)S(1)} fusion(f32[1440,768]{1,0:T(8,128)} %copy-done.6, bf16[1440,3072]{1,0:T(8,128)(2,1)} %get-tuple-element.75, bf16[3072,768]{0,1:T(8,128)(2,1)} %bitcast.181, f32[768]{0:T(1024)S(1)} %reshape.383), kind=kOutput, calls=%fused_computation.71 | convolution fusion | flops 6798090240 | bytes 20204544 | tf_op jit(solution)/shard_map/dot_general | solution.py:185
  723.6 11.4 %fusion.131 = (f32[768]{0:T(1024)S(1)}, f32[1440]{0:T(1024)S(1)}, f32[1440,768]{1,0:T(8,128)S(1)}) fusion(f32[768]{0:T(1024)S(1)} %copy-done.48, f32[1440]{0:T(1024)S(1)} %copy-done.37, bf16[640,768]{1,0:T(8,128)(2,1)S(1)} %bitcast.172, bf16[800,768]{1,0:T(8,128)(2,1)S(1)} %bitcast.156, bf16[768,2304]{1,0:T(8,128)(2,1)} %reshape.351, ...), kind=kOutput, calls=%fused_computation.185 | convolution fusion | flops 5119301120 | bytes 16827648 | tf_op jit(solution)/shard_map/tj,ij->ti/dot_general | solution.py:219
  749.7 39.8 %psum.7 = f32[9216]{0:T(1024)S(1)} all-reduce(f32[9216]{0:T(1024)S(1)} %constant_dynamic-update-slice_fusion), channel_id=1, replica_groups=mesh['img'=8,'seq'=4] {'img','seq'}, use_global_device_ids=true, to_apply=%region_22.23 | all-reduce | flops 9216 | bytes 73728 | tf_op jit(solution)/shard_map/psum | solution.py:234
  794.7 66.3 %reduce-scatter.5.cloned.1.call-done = bf16[1,1152,128]{2,1,0:T(8,128)(2,1)} async-done(((bf16[32,1152,128]{2,1,0:T(8,128)(2,1)}), bf16[1,1152,128]{2,1,0:T(8,128)(2,1)}) %reduce-scatter.5.cloned.1.call-update) | async-done | bytes 294928 | tf_op jit(solution)/shard_map/reduce_scatter | solution.py:99
  (301 shorter events, 373.7 us)
Async XLA Ops:
  7.2 15.2 %copy-start = (s32[64,40]{0,1:T(8,128)S(1)}, s32[64,40]{0,1:T(8,128)}, u32[]{:S(2)}) copy-start(s32[64,40]{0,1:T(8,128)} %param.21) | copy-start | bytes 30724
  7.2 15.3 %copy-start.10 = (bf16[16,40,768]{2,1,0:T(8,128)(2,1)S(1)}, bf16[16,40,768]{2,1,0:T(8,128)(2,1)}, u32[]{:S(2)}) copy-start(bf16[16,40,768]{2,1,0:T(8,128)(2,1)} %param.19) | copy-start | bytes 2949124
  7.2 15.3 %copy-start.4 = (bf16[4,200,768]{2,1,0:T(8,128)(2,1)S(1)}, bf16[4,200,768]{2,1,0:T(8,128)(2,1)}, u32[]{:S(2)}) copy-start(bf16[4,200,768]{2,1,0:T(8,128)(2,1)} %param.18) | copy-start | bytes 3686404
  7.2 73.8 %all-gather.7.cloned.1.call-start = ((), (), s32[]{:S(2)}) async-start(), calls=%async_computation.4 | async-start | bytes 4325376 | tf_op jit(solution)/shard_map/all_gather | solution.py:77
  16.0 205.4 %all-gather.9.cloned.1.call-start = ((), (), s32[]{:S(2)}) async-start(), calls=%async_computation.5 | async-start | bytes 11354112 | tf_op jit(solution)/shard_map/all_gather | solution.py:77
  22.3 769.2 %reduce-scatter.3.cloned.1.call-start = ((), (), s32[]{:S(2)}) async-start(), calls=%async_computation.2 | async-start | bytes 4866048 | tf_op jit(solution)/shard_map/reduce_scatter | solution.py:99
  23.6 185.4 %copy-start.51 = (pred[4,200]{1,0:T(4,128)(4,1)}, pred[4,200]{1,0:T(4,128)(4,1)S(1)}, u32[]{:S(2)}) copy-start(pred[4,200]{1,0:T(4,128)(4,1)S(1)} %dynamic-slice_compare_fusion) | copy-start | bytes 2404
  23.6 98.3 %copy-start.36 = (f32[1440]{0:T(1024)}, f32[1440]{0:T(1024)S(1)}, u32[]{:S(2)}) copy-start(f32[1440]{0:T(1024)S(1)} %broadcast_multiply_fusion.1) | copy-start | bytes 17284
  25.0 96.9 %copy-start.38 = (f32[1440]{0:T(1024)}, f32[1440]{0:T(1024)S(1)}, u32[]{:S(2)}) copy-start(f32[1440]{0:T(1024)S(1)} %fusion.103) | copy-start | bytes 17284
  84.5 37.5 %copy-start.53 = (f32[768]{0:T(1024)}, f32[768]{0:T(1024)S(1)}, u32[]{:S(2)}) copy-start(f32[768]{0:T(1024)S(1)} %reshape.378) | copy-start | bytes 9220
  84.7 37.3 %copy-start.47 = (f32[768]{0:T(1024)}, f32[768]{0:T(1024)S(1)}, u32[]{:S(2)}) copy-start(f32[768]{0:T(1024)S(1)} %reshape.377) | copy-start | bytes 9220
  136.4 191.7 %copy-start.55 = (f32[768]{0:T(1024)}, f32[768]{0:T(1024)S(1)}, u32[]{:S(2)}) copy-start(f32[768]{0:T(1024)S(1)} %reshape.381) | copy-start | bytes 9220
  324.6 51.7 %slice-start.2 = ((s8[4718592]{0:T(1024)(128)(4,1)}), s8[524288]{0:T(1024)(128)(4,1)S(1)}, s32[]{:S(2)}) async-start(s8[4718592]{0:T(1024)(128)(4,1)} %bitcast.182), calls=%async_computation.8 | async-start | bytes 1048576
  327.4 83.9 %copy-start.6 = (f32[1440,768]{1,0:T(8,128)}, f32[1440,768]{1,0:T(8,128)S(1)}, u32[]{:S(2)}) copy-start(f32[1440,768]{1,0:T(8,128)S(1)} %get-tuple-element.108) | copy-start | bytes 13271044
  328.1 48.2 %copy-start.44 = (f32[1440]{0:T(1024)}, f32[1440]{0:T(1024)S(1)}, u32[]{:S(2)}) copy-start(f32[1440]{0:T(1024)S(1)} %multiply_reduce_fusion.3) | copy-start | bytes 17284
  328.1 48.2 %copy-start.19 = (bf16[4,200,768]{2,1,0:T(8,128)(2,1)S(1)}, bf16[4,200,768]{2,1,0:T(8,128)(2,1)}, u32[]{:S(2)}) copy-start(bf16[4,200,768]{2,1,0:T(8,128)(2,1)} %param.34) | copy-start | bytes 3686404
  328.1 48.2 %slice-start.3 = ((s8[4718592]{0:T(1024)(128)(4,1)}), s8[4194304]{0:T(1024)(128)(4,1)S(1)}, s32[]{:S(2)}) async-start(s8[4718592]{0:T(1024)(128)(4,1)} %bitcast.182), calls=%async_computation.9 | async-start | bytes 8388608
  475.5 19.7 %copy-start.15 = (bf16[4,200,1,12,64]{1,4,3,0,2:T(8,128)(2,1)S(1)}, bf16[4,200,1,12,64]{1,4,3,0,2:T(8,128)(2,1)}, u32[]{:S(2)}) copy-start(bf16[4,200,1,12,64]{1,4,3,0,2:T(8,128)(2,1)} %copy.213) | copy-start | bytes 3686404
  495.2 19.0 %copy-start.32 = (bf16[768,768]{1,0:T(8,128)(2,1)S(1)}, bf16[768,768]{1,0:T(8,128)(2,1)}, u32[]{:S(2)}) copy-start(bf16[768,768]{1,0:T(8,128)(2,1)} %convolution_convert_fusion.4) | copy-start | bytes 3538948
  613.6 247.5 %reduce-scatter.5.cloned.1.call-start = ((), (), s32[]{:S(2)}) async-start(), calls=%async_computation.3 | async-start | bytes 9732096 | tf_op jit(solution)/shard_map/reduce_scatter | solution.py:99
  708.4 15.2 %copy-start.7 = (bf16[800,2304]{0,1:T(8,128)(2,1)S(1)}, bf16[800,2304]{0,1:T(8,128)(2,1)}, u32[]{:S(2)}) copy-start(bf16[800,2304]{0,1:T(8,128)(2,1)} %convert_element_type.280) | copy-start | bytes 11059204
  722.5 16.6 %slice-start = ((s8[4423680]{0:T(1024)(128)(4,1)}), s8[4194304]{0:T(1024)(128)(4,1)S(1)}, s32[]{:S(2)}) async-start(s8[4423680]{0:T(1024)(128)(4,1)} %bitcast.148), calls=%async_computation.6 | async-start | bytes 8388608
  723.6 15.5 %slice-start.1 = ((s8[4423680]{0:T(1024)(128)(4,1)}), s8[229376]{0:T(1024)(128)(4,1)S(1)}, s32[]{:S(2)}) async-start(s8[4423680]{0:T(1024)(128)(4,1)} %bitcast.148), calls=%async_computation.7 | async-start | bytes 458752
  745.3 118.5 %copy-start.1 = (s32[64,40]{0,1:T(8,128)S(1)}, s32[64,40]{0,1:T(8,128)}, u32[]{:S(2)}) copy-start(s32[64,40]{0,1:T(8,128)} %param.21) | copy-start | bytes 30724
  (43 other events, 238.0 us)
Sparse Core Ops, SparseCore 0:
  16.2 64.7 all-gather.6
  84.4 87.4 all-gather.8
  613.7 105.7 reduce-scatter.2
  726.2 134.7 reduce-scatter.4
